TPU v7x, 512 devices: a whole 4x4x16 slice. The times are simulated.
512 devices in a mesh: frames: 64 (over z, y), strips: 8 (over x, core).
Axes of the slice: x: 4, y: 4, z: 16, core: 2. Of those that a mesh axis runs over, the one named last changes fastest.
Arguments:
- raw_frames: bfloat16 [4096, 512, 512], P('frames', 'strips'), may hold values from -24 to 24
- dark_frame: float32 [512, 512], P('strips'), may hold values from -6 to 6
- dead_mask: int32 [512, 512], P('strips'), may hold values 0 or 1
- frame_group: int32 [4096], P('frames'), may hold values from 0 to 7
- prior_sigma: float32 [128], replicated, may hold values from 0.2 to 0.5
- start_rotation: float32 [128, 128], replicated, as said below
- basis: bfloat16 [262144, 128], P(('strips', 'frames')), may hold values from -0.01171875 to 0.01171875
Outputs:
- new_basis: bfloat16 [262144, 128], P(('strips', 'frames'))
- new_coeffs: float32 [4096, 128], P('frames')
- new_sigma: float32 [128], replicated
Inputs may be any that keep to these rules, and one draw needn't show every extreme that they name: start_rotation is nonsingular.
All inputs are finite; a program needn't handle non-finite values. No bound on the sum of `dead_mask` on one device may be relied on, other than what follows from the above.
Results may differ from a plain program's by a relative error of at most 0.0071.
Values may be sent and summed in bfloat16 or wider, within the bound.
A program may use at most 64 MiB of HBM per device.

v0:
```python
import jax
import jax.numpy as jnp
from jax import lax
from jax.sharding import PartitionSpec as P

GROUPS = 8
ITERS = 4
BLUR_TAPS = (1.0 / 64, 6.0 / 64, 15.0 / 64, 20.0 / 64, 15.0 / 64, 6.0 / 64, 1.0 / 64)
DECAY_RATE = 0.7


def extended(shard, sides, width):
    for axis, dim in sides:
        size, length = (lax.axis_size(axis), shard.shape[dim])
        up = [(i, (i + 1) % size) for i in range(size - 1)]
        down = [(j, i) for i, j in up]
        last = lax.slice_in_dim(shard, length - width, length, axis=dim)
        first = lax.slice_in_dim(shard, 0, width, axis=dim)
        before = lax.ppermute(last, axis, up)
        after = lax.ppermute(first, axis, down)
        shard = jnp.concatenate([before, shard, after], axis=dim)
    return shard


def orthonormalize(product):
    normal = jnp.dot(product.T, product, precision=lax.Precision.HIGHEST)
    factor = jnp.linalg.cholesky(normal)
    return lax.linalg.triangular_solve(
        factor, product, left_side=False, lower=True, transpose_a=True
    )


def body(raw_frames, dark_frame, dead_mask, frame_group, prior_sigma, start_rotation, basis):
    frame_count, strip_rows, columns = raw_frames.shape
    corrected = (
        (raw_frames.astype(jnp.float32) - dark_frame) * (1 - dead_mask).astype(jnp.float32)
    ).astype(jnp.bfloat16)
    position = jnp.arange(columns)
    offsets = position[None, :] - position[:, None]
    banded = jnp.zeros((columns, columns), jnp.float32)
    for shift_by in range(-3, 4):
        banded = banded + jnp.where(offsets == shift_by, BLUR_TAPS[shift_by + 3], 0.0)
    banded = banded.astype(jnp.bfloat16)
    column_blur = jnp.dot(
        corrected.reshape(frame_count * strip_rows, columns),
        banded,
        preferred_element_type=jnp.float32,
    )
    column_blur = column_blur.reshape(frame_count, strip_rows, columns)
    padded = extended(column_blur, (("strips", 1),), 3)
    row_blur = BLUR_TAPS[0] * padded[:, 0:strip_rows, :]
    for offset in range(1, 7):
        row_blur = row_blur + BLUR_TAPS[offset] * padded[:, offset : offset + strip_rows, :]
    frame_weight = jnp.power(
        jnp.float32(DECAY_RATE), (GROUPS - 1 - frame_group).astype(jnp.float32)
    )
    weighted = (
        (frame_weight[:, None, None] * row_blur)
        .astype(jnp.bfloat16)
        .reshape(frame_count, strip_rows * columns)
    )
    partial_value = jnp.dot(
        weighted,
        lax.all_gather(basis, "frames", axis=0, tiled=True),
        preferred_element_type=jnp.float32,
    )
    coeffs = lax.psum(partial_value, "strips")
    total_frames = frame_count * lax.axis_size("frames")
    local_gram = jnp.dot(coeffs.T, coeffs, precision=lax.Precision.HIGHEST)
    summed_gram = lax.psum(local_gram, "frames")
    gram = jnp.diag(prior_sigma * prior_sigma) + summed_gram / total_frames
    rotation = start_rotation
    for step in range(ITERS):
        rotation = orthonormalize(jnp.dot(gram, rotation, precision=lax.Precision.HIGHEST))
    new_coeffs = jnp.dot(coeffs, rotation, precision=lax.Precision.HIGHEST)
    new_basis = jnp.dot(
        basis.astype(jnp.float32), rotation, precision=lax.Precision.HIGHEST
    ).astype(jnp.bfloat16)
    curved = jnp.dot(gram, rotation, precision=lax.Precision.HIGHEST)
    new_sigma = jnp.sqrt(jnp.sum(rotation * curved, axis=0))
    return (new_basis, new_coeffs, new_sigma)


def solution(mesh):
    placed = (
        P("frames", "strips", None),
        P("strips", None),
        P("strips", None),
        P("frames"),
        P(),
        P(),
        P(("strips", "frames"), None),
    )
    return jax.shard_map(
        body,
        mesh=mesh,
        in_specs=placed,
        out_specs=(P(("strips", "frames"), None), P("frames", None), P()),
        check_vma=False,
    )
```

profile of v0, /device:TPU:2, one launch (start us, length us, event | category | flops | bytes accessed | tf_op | source)
XLA Modules:
  0.0 562.9 jit_solution(2204300600447689643)
XLA Ops:
  7.2 0.0 copy-start
  7.2 0.0 all-gather.2.cloned.1.call-start
  7.2 0.7 all-gather.2.cloned.1.call-update
  7.9 0.0 all-reduce.2.cloned.1.call-start
  8.0 0.9 subtract_convert_fusion
  8.9 0.0 copy-start.2
  8.9 4.7 fusion.18
  13.6 0.2 fusion.85
  13.9 1.9 collective-permute-start
  15.8 3.6 collective-permute-start.1
  19.5 0.0 copy-done.2
  19.5 4.9 collective-permute-done
  24.4 1.8 collective-permute-done.1
  26.1 8.9 %fusion.5 = bf16[64,64,512]{2,1,0:T(8,128)(2,1)S(1)} fusion(f32[64,64,512]{2,1,0:T(8,128)S(1)} %fusion.18, f32[64,3,512]{2,1,0:T(4,128)S(1)} %collective-permute-done.1, f32[64,3,512]{2,1,0:T(4,128)S(1)} %collective-permute-done, f32[64]{0:T(128)S(1)} %convert_power_fusion), kind=kLoop, calls=%fused_computation.13 | loop fusion | flops 44040192 | bytes 13369600 | tf_op jit(solution)/shard_map/convert_element_type | solution.py:59
  35.0 4.5 copy.15
  39.6 132.9 %all-gather.2.cloned.1.call-done = bf16[32768,128]{1,0:T(8,128)(2,1)} async-done(((bf16[512,128]{1,0:T(8,128)(2,1)}), bf16[32768,128]{1,0:T(8,128)(2,1)}) %all-gather.2.cloned.1.call-update) | async-done | bytes 8388624 | tf_op jit(solution)/shard_map/all_gather | solution.py:64
  172.4 0.0 copy-start.3
  172.4 0.0 copy-start.1
  172.4 6.3 %fusion.86 = f32[64,128]{1,0:T(8,128)S(1)} fusion(bf16[64,32768]{1,0:T(8,128)(2,1)} %bitcast.76, bf16[32768,128]{1,0:T(8,128)(2,1)} %all-gather.2.cloned.1.call-done), kind=kOutput, calls=%fused_computation.116 | convolution fusion | flops 536870912 | bytes 12615680 | tf_op jit(solution)/shard_map/dot_general | solution.py:62
  178.7 20.7 %psum.14 = f32[64,128]{1,0:T(8,128)S(1)} all-reduce(f32[64,128]{1,0:T(8,128)S(1)} %fusion.86), channel_id=1, replica_groups=mesh['frames'=64,'strips'=8] {'strips'}, use_global_device_ids=true, to_apply=%region_0.1 | all-reduce | flops 8192 | bytes 65536 | tf_op jit(solution)/shard_map/psum | solution.py:67
  199.4 0.9 fusion.87
  200.3 0.0 all-reduce.2.cloned.1.call-update
  200.3 0.0 copy-done.3
  200.4 253.0 %all-reduce.2.cloned.1.call-done = f32[128,128]{1,0:T(8,128)} async-done(((f32[128,128]{1,0:T(8,128)}), f32[128,128]{1,0:T(8,128)}) %all-reduce.2.cloned.1.call-update) | async-done | bytes 65552 | tf_op jit(solution)/shard_map/psum | solution.py:70
  453.4 0.0 copy-done
  453.4 1.1 fusion.83
  454.5 0.3 fusion.88
  454.8 0.1 copy.10
  454.9 11.7 %cholesky.74 = f32[128,128]{1,0:T(8,128)S(1)} custom-call(f32[128,128]{1,0:T(8,128)S(1)} %fusion.55), custom_call_target="Cholesky" | custom-call | tf_op jit(solution)/shard_map/jit(cholesky)/cholesky | solution.py:27
  466.6 0.6 compare_reduce_fusion.3
  467.3 0.7 fusion.44
  468.0 9.8 %custom-call.8 = f32[1,128,128]{1,2,0:T(8,128)S(1)} custom-call(f32[1,128,128]{2,1,0:T(8,128)S(1)} %fusion.44), custom_call_target="InvertDiagBlocksLowerTriangular" | custom-call | tf_op jit(solution)/shard_map/triangular_solve/custom-call.0 | solution.py:28
  477.8 0.3 convolution_bitcast_fusion.3
  478.1 1.1 fusion.81
  479.2 0.3 fusion.89
  479.5 0.1 copy.11
  479.6 11.7 %cholesky.85 = f32[128,128]{1,0:T(8,128)S(1)} custom-call(f32[128,128]{1,0:T(8,128)S(1)} %fusion.53), custom_call_target="Cholesky" | custom-call | tf_op jit(solution)/shard_map/jit(cholesky)/cholesky | solution.py:27
  491.4 0.6 compare_reduce_fusion.2
  492.0 0.7 fusion.45
  492.7 10.0 %custom-call.9 = f32[1,128,128]{1,2,0:T(8,128)S(1)} custom-call(f32[1,128,128]{2,1,0:T(8,128)S(1)} %fusion.45), custom_call_target="InvertDiagBlocksLowerTriangular" | custom-call | tf_op jit(solution)/shard_map/triangular_solve/custom-call.0 | solution.py:28
  502.7 0.3 convolution_bitcast_fusion.2
  503.0 1.1 fusion.79
  504.1 0.3 fusion.90
  504.4 0.1 copy.12
  504.5 11.7 %cholesky.96 = f32[128,128]{1,0:T(8,128)S(1)} custom-call(f32[128,128]{1,0:T(8,128)S(1)} %fusion.51), custom_call_target="Cholesky" | custom-call | tf_op jit(solution)/shard_map/jit(cholesky)/cholesky | solution.py:27
  516.3 0.6 compare_reduce_fusion.1
  516.9 0.7 fusion.46
  517.6 9.8 %custom-call.10 = f32[1,128,128]{1,2,0:T(8,128)S(1)} custom-call(f32[1,128,128]{2,1,0:T(8,128)S(1)} %fusion.46), custom_call_target="InvertDiagBlocksLowerTriangular" | custom-call | tf_op jit(solution)/shard_map/triangular_solve/custom-call.0 | solution.py:28
  527.4 0.3 convolution_bitcast_fusion.1
  527.7 1.1 fusion.77
  528.8 0.3 fusion.91
  529.1 0.1 copy.13
  529.2 11.7 %cholesky.107 = f32[128,128]{1,0:T(8,128)S(1)} custom-call(f32[128,128]{1,0:T(8,128)S(1)} %fusion.49), custom_call_target="Cholesky" | custom-call | tf_op jit(solution)/shard_map/jit(cholesky)/cholesky | solution.py:27
  541.0 0.6 compare_reduce_fusion
  541.6 0.7 fusion.47
  542.3 10.0 %custom-call.11 = f32[1,128,128]{1,2,0:T(8,128)S(1)} custom-call(f32[1,128,128]{2,1,0:T(8,128)S(1)} %fusion.47), custom_call_target="InvertDiagBlocksLowerTriangular" | custom-call | tf_op jit(solution)/shard_map/triangular_solve/custom-call.0 | solution.py:28
  552.3 0.2 convolution_bitcast_fusion
  552.5 0.8 fusion.92
  553.3 0.0 copy-done.1
  553.3 0.3 fusion.21
  553.6 1.1 fusion.22
  554.7 0.5 sqrt.3
  555.3 0.8 copy.14
  (10 shorter events, 0.2 us)
Async XLA Ops:
  7.2 446.2 %copy-start = (f32[128,128]{1,0:T(8,128)S(1)}, f32[128,128]{1,0:T(8,128)}, u32[]{:S(2)}) copy-start(f32[128,128]{1,0:T(8,128)} %param.15) | copy-start | bytes 196612
  7.2 165.3 %all-gather.2.cloned.1.call-start = ((), (), s32[]{:S(2)}) async-start(), calls=%async_computation | async-start | bytes 8519680 | tf_op jit(solution)/shard_map/all_gather | solution.py:64
  7.9 445.5 %all-reduce.2.cloned.1.call-start = ((), (), s32[]{:S(2)}) async-start(), calls=%async_computation.1 | async-start | bytes 131072 | tf_op jit(solution)/shard_map/psum | solution.py:70
  8.9 10.6 %copy-start.2 = (s32[64]{0:T(128)S(1)}, s32[64]{0:T(128)}, u32[]{:S(2)}) copy-start(s32[64]{0:T(128)} %param.13) | copy-start | bytes 772
  13.9 10.5 %collective-permute-start = (f32[64,3,512]{2,1,0:T(4,128)S(1)}, f32[64,3,512]{2,1,0:T(4,128)S(1)}, u32[]{:S(2)}, u32[]{:S(2)}) collective-permute-start(f32[64,3,512]{2,1,0:T(4,128)S(1)} %get-tuple-element.8), channel_id=1, source_target_pairs={{0,1},{1,2},{2,3},{3,4},{4,5},{5,6},{6,7},{8,9},{9,10},{10,11},{11... | collective-permute-start | bytes 1179656 | tf_op jit(solution)/shard_map/ppermute | solution.py:19
  15.8 10.3 %collective-permute-start.1 = (f32[64,3,512]{2,1,0:T(4,128)S(1)}, f32[64,3,512]{2,1,0:T(4,128)S(1)}, u32[]{:S(2)}, u32[]{:S(2)}) collective-permute-start(f32[64,3,512]{2,1,0:T(4,128)S(1)} %get-tuple-element.9), channel_id=1, source_target_pairs={{1,0},{2,1},{3,2},{4,3},{5,4},{6,5},{7,6},{9,8},{10,9},{11,10},{12... | collective-permute-start | bytes 1179656 | tf_op jit(solution)/shard_map/ppermute | solution.py:20
  172.4 27.9 %copy-start.3 = (f32[128]{0:T(128)S(1)}, f32[128]{0:T(128)}, u32[]{:S(2)}) copy-start(f32[128]{0:T(128)} %param.14) | copy-start | bytes 1540
  172.4 380.9 %copy-start.1 = (bf16[512,128]{1,0:T(8,128)(2,1)S(1)}, bf16[512,128]{1,0:T(8,128)(2,1)}, u32[]{:S(2)}) copy-start(bf16[512,128]{1,0:T(8,128)(2,1)} %param.16) | copy-start | bytes 393220
Sparse Core Ops, SparseCore 0:
  11.0 161.4 all-gather.1
  200.5 252.8 all-reduce.1
where the time goes:
time: 563 us
  waiting for transfers between devices  393 us (70%)
  other arithmetic  102 us (18%)
  matrix products  20.9 us (4%)
  blocking collectives  20.7 us (4%)
  between operations  14.3 us (3%)
  local copies, waits for them, and re-layouts  6.45 us (1%)
  starting transfers between devices  5.64 us (1%)
    psum x1, waiting for transfers between devices, body(): summed_gram = lax.psum(local_gram, 'frames')  253 us
    all_gather x1, waiting for transfers between devices, body(): lax.all_gather(basis, 'frames', axis=0, tiled=True)  133 us
    another operation x12, other arithmetic, orthonormalize(): factor = jnp.linalg.cholesky(normal)  49.6 us
    another operation x8, other arithmetic, orthonormalize(): lax.linalg.triangular_solve(factor, product, left_side=False, lower=True,...  42.2 us
    psum x1, blocking collectives, body(): coeffs = lax.psum(partial_value, 'strips')  20.7 us
  transfers between devices with their start and end apart: 4, of which 4 were waited for; matrix products, arithmetic and copies ran while one was open for 3% of the time, Pallas kernels for 0%

commit v1 on v0

--- a/solution.py
+++ b/solution.py
@@ -61,7 +61,12 @@
     )
     partial_value = jnp.dot(
         weighted,
-        lax.all_gather(basis, "frames", axis=0, tiled=True),
+        jnp.concatenate(
+            lax.all_to_all(
+                jnp.stack([basis] * lax.psum(1, "frames")), "frames", split_axis=0, concat_axis=0
+            ),
+            0,
+        ),
         preferred_element_type=jnp.float32,
     )
     coeffs = lax.psum(partial_value, "strips")

time: 563 us -> 804 us (1.43); the launches traced: 563 us -> 795 us
  waiting for transfers between devices: 393 us -> 601 us
  starting transfers between devices: 5.64 us -> 24.7 us
    all_to_all x0 -> x1, waiting for transfers between devices: none -> 343 us  [body(): lax.all_to_all(jnp.stack([basis] * lax.psum(1, 'frames')), 'frames', spli...]
    all_gather x1 -> x0, waiting for transfers between devices: 133 us -> none  [body(): lax.all_gather(basis, 'frames', axis=0, tiled=True)]
    all_to_all x0 -> x1, starting transfers between devices: none -> 19.1 us  [body(): lax.all_to_all(jnp.stack([basis] * lax.psum(1, 'frames')), 'frames', spli...]
  transfers between devices with their start and end apart: 4 -> 4, of which waited for: 4 -> 4; matrix products, arithmetic and copies ran while one was open for 3% -> 2% of each run, Pallas kernels for 0% -> 0%
where the time goes in v1:
time: 804 us; the launch traced here: 795 us
  waiting for transfers between devices  601 us (75%)
  other arithmetic  102 us (13%)
  starting transfers between devices  24.7 us (3%)
  matrix products  24.4 us (3%)
  blocking collectives  20.8 us (3%)
  between operations  14.8 us (2%)
  local copies, waits for them, and re-layouts  8.09 us (1%)
    all_to_all x1, waiting for transfers between devices, body(): lax.all_to_all(jnp.stack([basis] * lax.psum(1, 'frames')), 'frames', spli...  343 us
    psum x1, waiting for transfers between devices, body(): summed_gram = lax.psum(local_gram, 'frames')  251 us
    another operation x12, other arithmetic, orthonormalize(): factor = jnp.linalg.cholesky(normal)  49.6 us
    another operation x8, other arithmetic, orthonormalize(): lax.linalg.triangular_solve(factor, product, left_side=False, lower=True,...  42.3 us
    psum x1, blocking collectives, body(): coeffs = lax.psum(partial_value, 'strips')  20.8 us
    all_to_all x1, starting transfers between devices, body(): lax.all_to_all(jnp.stack([basis] * lax.psum(1, 'frames')), 'frames', spli...  19.1 us
  transfers between devices with their start and end apart: 4, of which 4 were waited for; matrix products, arithmetic and copies ran while one was open for 2% of the time, Pallas kernels for 0%

profile of v1, /device:TPU:2, one launch (start us, length us, event | category | flops | bytes accessed | tf_op | source)
XLA Modules:
  0.0 795.2 jit_solution(4203248741519737138)
XLA Ops:
  7.2 0.0 copy-start
  7.2 6.2 stack.2
  13.3 0.0 copy-start.2
  13.4 0.0 copy-start.3
  13.4 19.1 %all-to-all-start = ((bf16[64,512,128]{2,1,0:T(8,128)(2,1)}), bf16[64,512,128]{2,1,0:T(8,128)(2,1)}, u32[]{:S(2)}, u32[]{:S(2)}) async-start(bf16[64,512,128]{2,1,0:T(8,128)(2,1)} %stack.2), calls=%async_computation | async-start | bytes 16777216 | tf_op jit(solution)/shard_map/all_to_all | solution.py:65
  32.5 0.0 all-reduce.2.cloned.1.call-start
  32.5 0.0 copy-done.2
  32.6 0.0 copy-done.3
  32.6 0.0 copy-start.4
  32.6 4.8 fusion.18
  37.4 0.2 fusion.90
  37.6 1.9 collective-permute-start
  39.5 3.6 collective-permute-start.1
  43.2 0.0 copy-done.4
  43.2 4.9 collective-permute-done
  48.1 1.8 collective-permute-done.1
  49.9 9.7 %fusion.5 = bf16[64,64,512]{2,1,0:T(8,128)(2,1)} fusion(f32[64,64,512]{2,1,0:T(8,128)S(1)} %fusion.18, f32[64,3,512]{2,1,0:T(4,128)S(1)} %collective-permute-done.1, f32[64,3,512]{2,1,0:T(4,128)S(1)} %collective-permute-done, f32[64]{0:T(128)S(1)} %convert_power_fusion), kind=kLoop, calls=%fused_computation.13 | loop fusion | flops 44040192 | bytes 13369600 | tf_op jit(solution)/shard_map/convert_element_type | solution.py:59
  59.6 0.0 copy-start.5
  59.6 342.7 %all-to-all-done = bf16[64,512,128]{2,1,0:T(8,128)(2,1)} async-done(((bf16[64,512,128]{2,1,0:T(8,128)(2,1)}), bf16[64,512,128]{2,1,0:T(8,128)(2,1)}, u32[]{:S(2)}, u32[]{:S(2)}) %all-to-all-start) | async-done | bytes 8388640 | tf_op jit(solution)/shard_map/all_to_all | solution.py:65
  402.3 9.8 %fusion.25 = f32[64,128]{1,0:T(8,128)S(1)} fusion(bf16[64,512,128]{2,1,0:T(8,128)(2,1)} %all-to-all-done, bf16[64,64,512]{2,1,0:T(8,128)(2,1)} %fusion.5), kind=kOutput, calls=%fused_computation.42 | convolution fusion | flops 536870912 | bytes 12615680 | tf_op jit(solution)/shard_map/dot_general | solution.py:62
  412.0 20.8 %psum.14 = f32[64,128]{1,0:T(8,128)S(1)} all-reduce(f32[64,128]{1,0:T(8,128)S(1)} %fusion.25), channel_id=1, replica_groups=mesh['frames'=64,'strips'=8] {'strips'}, use_global_device_ids=true, to_apply=%region_0.1 | all-reduce | flops 8192 | bytes 65536 | tf_op jit(solution)/shard_map/psum | solution.py:72
  432.8 0.9 fusion.91
  433.8 0.0 all-reduce.2.cloned.1.call-update
  433.8 0.0 copy-done.5
  433.8 251.5 %all-reduce.2.cloned.1.call-done = f32[128,128]{1,0:T(8,128)} async-done(((f32[128,128]{1,0:T(8,128)}), f32[128,128]{1,0:T(8,128)}) %all-reduce.2.cloned.1.call-update) | async-done | bytes 65552 | tf_op jit(solution)/shard_map/psum | solution.py:75
  685.3 0.0 copy-done
  685.3 1.1 fusion.88
  686.4 0.3 fusion.92
  686.7 0.1 copy.11
  686.8 11.7 %cholesky.74 = f32[128,128]{1,0:T(8,128)S(1)} custom-call(f32[128,128]{1,0:T(8,128)S(1)} %fusion.60), custom_call_target="Cholesky" | custom-call | tf_op jit(solution)/shard_map/jit(cholesky)/cholesky | solution.py:27
  698.5 0.6 compare_reduce_fusion.3
  699.2 0.7 fusion.49
  699.8 9.8 %custom-call.8 = f32[1,128,128]{1,2,0:T(8,128)S(1)} custom-call(f32[1,128,128]{2,1,0:T(8,128)S(1)} %fusion.49), custom_call_target="InvertDiagBlocksLowerTriangular" | custom-call | tf_op jit(solution)/shard_map/triangular_solve/custom-call.0 | solution.py:28
  709.7 0.3 convolution_bitcast_fusion.3
  709.9 1.1 fusion.86
  711.1 0.3 fusion.93
  711.4 0.1 copy.12
  711.5 11.7 %cholesky.85 = f32[128,128]{1,0:T(8,128)S(1)} custom-call(f32[128,128]{1,0:T(8,128)S(1)} %fusion.58), custom_call_target="Cholesky" | custom-call | tf_op jit(solution)/shard_map/jit(cholesky)/cholesky | solution.py:27
  723.2 0.6 compare_reduce_fusion.2
  723.9 0.7 fusion.50
  724.6 10.0 %custom-call.9 = f32[1,128,128]{1,2,0:T(8,128)S(1)} custom-call(f32[1,128,128]{2,1,0:T(8,128)S(1)} %fusion.50), custom_call_target="InvertDiagBlocksLowerTriangular" | custom-call | tf_op jit(solution)/shard_map/triangular_solve/custom-call.0 | solution.py:28
  734.6 0.3 convolution_bitcast_fusion.2
  734.8 1.1 fusion.84
  736.0 0.3 fusion.94
  736.3 0.1 copy.13
  736.4 11.7 %cholesky.96 = f32[128,128]{1,0:T(8,128)S(1)} custom-call(f32[128,128]{1,0:T(8,128)S(1)} %fusion.56), custom_call_target="Cholesky" | custom-call | tf_op jit(solution)/shard_map/jit(cholesky)/cholesky | solution.py:27
  748.1 0.6 compare_reduce_fusion.1
  748.8 0.7 fusion.51
  749.5 9.8 %custom-call.10 = f32[1,128,128]{1,2,0:T(8,128)S(1)} custom-call(f32[1,128,128]{2,1,0:T(8,128)S(1)} %fusion.51), custom_call_target="InvertDiagBlocksLowerTriangular" | custom-call | tf_op jit(solution)/shard_map/triangular_solve/custom-call.0 | solution.py:28
  759.3 0.3 convolution_bitcast_fusion.1
  759.6 1.1 fusion.82
  760.7 0.3 fusion.95
  761.0 0.1 copy.14
  761.1 11.7 %cholesky.107 = f32[128,128]{1,0:T(8,128)S(1)} custom-call(f32[128,128]{1,0:T(8,128)S(1)} %fusion.54), custom_call_target="Cholesky" | custom-call | tf_op jit(solution)/shard_map/jit(cholesky)/cholesky | solution.py:27
  772.9 0.6 compare_reduce_fusion
  773.5 0.7 fusion.52
  774.2 10.0 %custom-call.11 = f32[1,128,128]{1,2,0:T(8,128)S(1)} custom-call(f32[1,128,128]{2,1,0:T(8,128)S(1)} %fusion.52), custom_call_target="InvertDiagBlocksLowerTriangular" | custom-call | tf_op jit(solution)/shard_map/triangular_solve/custom-call.0 | solution.py:28
  784.2 0.2 convolution_bitcast_fusion
  784.4 0.8 fusion.96
  785.2 0.0 copy-done.1
  785.2 0.3 fusion.23
  785.6 1.1 fusion.24
  786.7 0.5 sqrt.3
  787.2 0.8 copy.15
  (12 shorter events, 0.2 us)
Async XLA Ops:
  7.2 678.1 %copy-start = (f32[128,128]{1,0:T(8,128)S(1)}, f32[128,128]{1,0:T(8,128)}, u32[]{:S(2)}) copy-start(f32[128,128]{1,0:T(8,128)} %param.15) | copy-start | bytes 196612
  13.3 19.2 %copy-start.2 = (s32[64,512]{1,0:T(8,128)S(1)}, s32[64,512]{1,0:T(8,128)}, u32[]{:S(2)}) copy-start(s32[64,512]{1,0:T(8,128)} %param.12) | copy-start | bytes 393220
  13.4 19.2 %copy-start.3 = (f32[64,512]{1,0:T(8,128)S(1)}, f32[64,512]{1,0:T(8,128)}, u32[]{:S(2)}) copy-start(f32[64,512]{1,0:T(8,128)} %param.11) | copy-start | bytes 393220
  13.4 388.9 %all-to-all-start = ((bf16[64,512,128]{2,1,0:T(8,128)(2,1)}), bf16[64,512,128]{2,1,0:T(8,128)(2,1)}, u32[]{:S(2)}, u32[]{:S(2)}) async-start(bf16[64,512,128]{2,1,0:T(8,128)(2,1)} %stack.2), calls=%async_computation | async-start | bytes 16777216 | tf_op jit(solution)/shard_map/all_to_all | solution.py:65
  32.5 652.8 %all-reduce.2.cloned.1.call-start = ((), (), s32[]{:S(2)}) async-start(), calls=%async_computation.1 | async-start | bytes 131072 | tf_op jit(solution)/shard_map/psum | solution.py:75
  32.6 10.6 %copy-start.4 = (s32[64]{0:T(128)S(1)}, s32[64]{0:T(128)}, u32[]{:S(2)}) copy-start(s32[64]{0:T(128)} %param.13) | copy-start | bytes 772
  37.6 10.5 %collective-permute-start = (f32[64,3,512]{2,1,0:T(4,128)S(1)}, f32[64,3,512]{2,1,0:T(4,128)S(1)}, u32[]{:S(2)}, u32[]{:S(2)}) collective-permute-start(f32[64,3,512]{2,1,0:T(4,128)S(1)} %get-tuple-element.8), channel_id=1, source_target_pairs={{0,1},{1,2},{2,3},{3,4},{4,5},{5,6},{6,7},{8,9},{9,10},{10,11},{11... | collective-permute-start | bytes 1179656 | tf_op jit(solution)/shard_map/ppermute | solution.py:19
  39.5 10.3 %collective-permute-start.1 = (f32[64,3,512]{2,1,0:T(4,128)S(1)}, f32[64,3,512]{2,1,0:T(4,128)S(1)}, u32[]{:S(2)}, u32[]{:S(2)}) collective-permute-start(f32[64,3,512]{2,1,0:T(4,128)S(1)} %get-tuple-element.9), channel_id=1, source_target_pairs={{1,0},{2,1},{3,2},{4,3},{5,4},{6,5},{7,6},{9,8},{10,9},{11,10},{12... | collective-permute-start | bytes 1179656 | tf_op jit(solution)/shard_map/ppermute | solution.py:20
  59.6 374.2 %copy-start.5 = (f32[128]{0:T(128)S(1)}, f32[128]{0:T(128)}, u32[]{:S(2)}) copy-start(f32[128]{0:T(128)} %param.14) | copy-start | bytes 1540
  59.6 725.6 %copy-start.1 = (bf16[512,128]{1,0:T(8,128)(2,1)S(1)}, bf16[512,128]{1,0:T(8,128)(2,1)}, u32[]{:S(2)}) copy-start(bf16[512,128]{1,0:T(8,128)(2,1)} %param.16) | copy-start | bytes 393220
Sparse Core Ops, SparseCore 0:
  433.9 251.3 all-reduce.1
